TPU v7x, 256 devices: a whole 4x4x8 slice. The times are simulated.
256 devices in a mesh: row: 8 (over x, core), col: 32 (over y, z).
Axes of the slice: x: 4, y: 4, z: 8, core: 2. Of those that a mesh axis runs over, the one named last changes fastest.
Arguments:
- hidden: bfloat16 [4096, 8192], P('row', 'col'), may hold values from -600 to 600
- norm_gain: float32 [8192], replicated, may hold values from 0.5 to 2
- wq: bfloat16 [8192, 8192], P('row', 'col'), may hold values from -1 to 1
- wk: bfloat16 [8192, 1024], P('row', 'col'), may hold values from -1 to 1
- wv: bfloat16 [8192, 1024], P('row', 'col'), may hold values from -0.0625 to 0.0625
- wo: bfloat16 [8192, 8192], P('row', 'col'), may hold values from -0.25 to 0.25
Outputs:
- attn_out: bfloat16 [4096, 8192], P('row', 'col')
All inputs are finite; a program needn't handle non-finite values.
Results may differ from a plain program's by a relative error of at most 0.011.
Values may be sent and summed in bfloat16 or wider, within the bound.
A program may use at most 64 MiB of HBM per device.

v0:
```python
import jax
import jax.numpy as jnp
from jax import lax
from jax.sharding import PartitionSpec as P

HD = 128


def partner(array, axis, distance):
    return lax.ppermute(array, axis, [(i, i ^ 1 << distance) for i in range(lax.axis_size(axis))])


def rotary(field, positions):
    half = field.shape[-1] // 2
    steps = jnp.arange(half).astype(jnp.float32)
    freqs = 10000.0 ** (-steps / half)
    angles = positions.astype(jnp.float32)[:, None] * freqs[None, :]
    cosine = jnp.cos(angles)[:, None, :]
    sine = jnp.sin(angles)[:, None, :]
    first = field[..., :half]
    second = field[..., half:]
    return jnp.concatenate(
        [first * cosine - second * sine, second * cosine + first * sine], axis=-1
    )


def order_pair(mine, other, col_index, bit, axis_dim):
    upper = col_index // 2**bit % 2 == 1
    lower_part = jnp.where(upper, other, mine)
    upper_part = jnp.where(upper, mine, other)
    return jnp.concatenate([lower_part, upper_part], axis=axis_dim)


def per_device(hidden, norm_gain, wq, wk, wv, wo):
    tok_rows = hidden.shape[0]
    panel = lax.all_gather(hidden, "col", axis=1, tiled=True)
    values_in = panel.astype(jnp.float32)
    meansq = jnp.mean(values_in * values_in, axis=1, keepdims=True)
    normed = (values_in * lax.rsqrt(meansq + 1e-05) * norm_gain).astype(jnp.bfloat16)
    kv_cols = wk.shape[1]
    group = max(1, HD // kv_cols)
    bits = group.bit_length() - 1
    col_index = lax.axis_index("col")
    stacked = jnp.stack((wk, wv), axis=1)
    for bit in range(bits):
        other = partner(stacked, "col", bit)
        stacked = order_pair(stacked, other, col_index, bit, 2)
    columns = normed
    query_part = jnp.dot(
        columns, lax.all_gather(wq, "row", axis=0, tiled=True), preferred_element_type=jnp.float32
    )
    pair_part = jnp.einsum(
        "ho,omr->hmr",
        columns,
        lax.all_gather(stacked, "row", axis=0, tiled=True),
        preferred_element_type=jnp.float32,
    )
    heads_here = wq.shape[1] // HD
    kv_here = pair_part.shape[2] // HD
    per_kv = heads_here // kv_here
    positions = lax.axis_index("row") * tok_rows + jnp.arange(tok_rows)
    queries = rotary(query_part.reshape(tok_rows, heads_here, HD), positions).astype(jnp.bfloat16)
    queries = queries.reshape(tok_rows, kv_here, per_kv, HD)
    keys = rotary(pair_part[:, 0].reshape(tok_rows, kv_here, HD), positions).astype(jnp.bfloat16)
    values = pair_part[:, 1].reshape(tok_rows, kv_here, HD).astype(jnp.bfloat16)
    scale = HD ** (-0.5)
    best = jnp.full((kv_here, per_kv, tok_rows), -1e30, jnp.float32)
    key_piece = lax.all_gather(keys, "row", axis=0, tiled=True)
    value_piece = lax.all_gather(values, "row", axis=0, tiled=True)
    count = key_piece.shape[0]
    scores = (
        jnp.einsum("tagd,nad->agtn", queries, key_piece, preferred_element_type=jnp.float32) * scale
    )
    key_pos = jnp.arange(count)
    visible = positions[:, None] >= key_pos[None, :]
    scores = jnp.where(visible, scores, -jnp.inf)
    fresh = jnp.maximum(best, jnp.max(scores, axis=3))
    probs = jnp.exp(scores - fresh[..., None])
    total = jnp.sum(probs, axis=3)
    update = jnp.einsum(
        "agtn,nad->agtd",
        probs.astype(jnp.bfloat16),
        value_piece,
        preferred_element_type=jnp.float32,
    )
    numer = update
    best, total, numer = (fresh, total, numer)
    heads = (
        (numer / total[..., None])
        .transpose(2, 0, 1, 3)
        .reshape(tok_rows, heads_here * HD)
        .astype(jnp.bfloat16)
    )
    head_panel = lax.all_gather(heads, "col", axis=1, tiled=True)
    columns = head_panel
    result = jnp.dot(
        columns, lax.all_gather(wo, "row", axis=0, tiled=True), preferred_element_type=jnp.float32
    )
    return result.astype(jnp.bfloat16)


def solution(mesh):
    in_specs = (
        P("row", "col"),
        P(),
        P("row", "col"),
        P("row", "col"),
        P("row", "col"),
        P("row", "col"),
    )
    out_specs = P("row", "col")
    return jax.shard_map(
        per_device, mesh=mesh, in_specs=in_specs, out_specs=out_specs, check_vma=False
    )
```

profile of v0, /device:TPU:1, one launch (start us, length us, event | category | flops | bytes accessed | tf_op | source)
XLA Modules:
  0.0 396.9 jit_solution(9538606364416327431)
XLA Ops:
  6.5 0.0 copy-start.1
  6.5 0.0 all-gather.8.cloned.1.call-start
  6.5 0.7 all-gather.8.cloned.1.call-update
  7.3 0.0 all-gather.10.cloned.1.call-start
  7.3 0.9 pad_maximum_fusion.2
  8.2 2.6 collective-permute-start
  10.7 2.4 collective-permute-done
  13.1 0.9 broadcast_select_fusion.3
  14.0 3.8 collective-permute-start.1
  17.9 11.3 %collective-permute-done.1 = bf16[1024,2,64]{0,2,1:T(8,128)(2,1)S(1)} collective-permute-done((bf16[1024,2,64]{0,2,1:T(8,128)(2,1)S(1)}, bf16[1024,2,64]{0,2,1:T(8,128)(2,1)S(1)}, u32[]{:S(2)}, u32[]{:S(2)}) %collective-permute-start.1) | collective-permute-done | bytes 262176 | tf_op jit(solution)/shard_map/ppermute | solution.py:10
  29.2 0.1 broadcast_select_fusion.1
  29.3 0.8 pad_maximum_fusion
  30.1 0.0 all-gather.10.cloned.1.call-update
  30.2 0.0 all-gather.14.cloned.1.call-start
  30.2 0.7 all-gather.14.cloned.1.call-update
  30.9 0.0 all-gather.12.cloned.1.call-start
  31.0 86.2 %all-gather.8.cloned.1.call-done = bf16[512,8192]{1,0:T(8,128)(2,1)} async-done(((bf16[512,256]{1,0:T(8,128)(2,1)}), bf16[512,8192]{1,0:T(8,128)(2,1)}) %all-gather.8.cloned.1.call-update) | async-done | bytes 8388624 | tf_op jit(solution)/shard_map/all_gather | solution.py:36
  117.1 5.1 %fusion = f32[512]{0:T(512)S(1)} fusion(bf16[512,8192]{1,0:T(8,128)(2,1)} %all-gather.8.cloned.1.call-done), kind=kLoop, calls=%fused_computation.2 | loop fusion | flops 12582400 | bytes 8390656 | tf_op jit(solution)/shard_map/reduce_sum | solution.py:38
  122.3 31.8 %all-gather.10.cloned.1.call-done = bf16[8192,2,128]{0,2,1:T(8,128)(2,1)} async-done(((bf16[1024,2,128]{0,2,1:T(8,128)(2,1)}), bf16[8192,2,128]{0,2,1:T(8,128)(2,1)}) %all-gather.10.cloned.1.call-update) | async-done | bytes 4194320 | tf_op jit(solution)/shard_map/all_gather | solution.py:55
  154.1 0.0 copy-done.1
  154.1 7.0 %fusion.12 = f32[512,256]{0,1:S(1)} fusion(bf16[8192,256]{0,1:T(8,128)(2,1)} %bitcast.61, bf16[512,8192]{1,0:T(8,128)(2,1)} %all-gather.8.cloned.1.call-done, f32[8192]{0:T(1024)S(1)} %copy-done.1, f32[512]{0:T(512)S(1)} %add_rsqrt_fusion), kind=kOutput, calls=%fused_computation.15 | convolution fusion | flops 2164260864 | bytes 13142016
  161.1 0.6 fusion.35
  161.7 0.7 pad_maximum_fusion.3
  162.4 0.0 all-gather.12.cloned.1.call-update
  162.4 0.0 all-gather.16.cloned.1.call-start
  162.4 0.7 slice.34
  163.1 0.0 all-gather.16.cloned.1.call-update
  163.1 0.0 all-gather.20.cloned.1.call-start
  163.2 0.5 all-gather.20.cloned.1.call-update
  163.7 0.2 all-gather.18.cloned.1.call-start
  163.9 1.8 multiply_cosine_fusion
  165.7 1.7 iota_compare_fusion
  167.5 23.2 %all-gather.14.cloned.1.call-done = bf16[8192,256]{1,0:T(8,128)(2,1)} async-done(((bf16[1024,256]{1,0:T(8,128)(2,1)}), bf16[8192,256]{1,0:T(8,128)(2,1)}) %all-gather.14.cloned.1.call-update) | async-done | bytes 4194320 | tf_op jit(solution)/shard_map/all_gather | solution.py:50
  190.6 7.6 %fusion.10 = f32[512,256]{0,1:T(8,128)S(1)} fusion(bf16[8192,256]{1,0:T(8,128)(2,1)} %all-gather.14.cloned.1.call-done, bf16[512,8192]{1,0:T(8,128)(2,1)} %all-gather.8.cloned.1.call-done, f32[8192]{0:T(1024)S(1)} %copy-done.1, f32[512]{0:T(512)S(1)} %add_rsqrt_fusion), kind=kOutput, calls=%fused_computation.14 | convolution fusion | flops 2164260864 | bytes 13142016 | tf_op jit(solution)/shard_map/dot_general | solution.py:49
  198.3 0.2 copy.14
  198.5 0.2 copy.15
  198.7 1.9 subtract_convert_fusion
  200.5 17.7 %all-gather.12.cloned.1.call-done = bf16[4096,1,128]{0,2,1:T(8,128)(2,1)} async-done(((bf16[512,1,128]{0,2,1:T(8,128)(2,1)}), bf16[4096,1,128]{0,2,1:T(8,128)(2,1)}) %all-gather.12.cloned.1.call-update) | async-done | bytes 1048592 | tf_op jit(solution)/shard_map/all_gather | solution.py:68
  218.2 5.1 %fusion.5 = (f32[2,512]{1,0:T(2,128)S(1)}, f32[4096,512,2]{1,0,2:T(8,128)S(1)}) fusion(pred[512,4096]{0,1:T(8,128)(4,1)S(1)} %iota_compare_fusion, bf16[512,2,64]{2,0,1:T(8,128)(2,1)} %get-tuple-element.6, bf16[512,2,64]{2,0,1:T(8,128)(2,1)S(1)} %get-tuple-element.5, bf16[4096,1,128]{0,2,1:T(8,128)(2,1)} %all-gather.12.cloned.1.call-done), kind=kOutput, calls=%fused_computation.9 | convolution fusion | flops 1086848000 | bytes 20189184 | tf_op jit(solution)/shard_map/tagd,nad->agtn/dot_general | solution.py:72
  223.3 0.0 copy-start
  223.3 5.7 %copy-done = f32[4096,512,2]{1,0,2:T(8,128)} copy-done((f32[4096,512,2]{1,0,2:T(8,128)}, f32[4096,512,2]{1,0,2:T(8,128)S(1)}, u32[]{:S(2)}) %copy-start) | copy-done | bytes 16777240
  229.0 4.2 %fusion.3 = f32[2,512]{1,0:T(2,128)S(1)} fusion(f32[4096,512,2]{1,0,2:T(8,128)S(1)} %get-tuple-element.18, f32[2,512]{1,0:T(2,128)S(1)} %broadcast_maximum_fusion, pred[512,4096]{0,1:T(8,128)(4,1)S(1)} %iota_compare_fusion), kind=kLoop, calls=%fused_computation.7 | loop fusion | flops 16776192 | bytes 18882560 | tf_op jit(solution)/shard_map/reduce_sum | solution.py:79
  233.2 12.6 %all-gather.16.cloned.1.call-done = bf16[4096,1,128]{0,2,1:T(8,128)(2,1)} async-done(((bf16[512,1,128]{0,2,1:T(8,128)(2,1)}), bf16[4096,1,128]{0,2,1:T(8,128)(2,1)}) %all-gather.16.cloned.1.call-update) | async-done | bytes 1048592 | tf_op jit(solution)/shard_map/all_gather | solution.py:69
  245.8 11.7 %fusion.22 = bf16[2,512,128]{1,2,0:T(8,128)(2,1)} fusion(f32[4096,512,2]{1,0,2:T(8,128)} %copy-done, f32[2,512]{1,0:T(2,128)S(1)} %broadcast_maximum_fusion, pred[512,4096]{0,1:T(8,128)(4,1)S(1)} %iota_compare_fusion, bf16[4096,1,128]{0,2,1:T(8,128)(2,1)} %all-gather.16.cloned.1.call-done, f32[2,512]{1,0:T(2,128)S(1)} %fusion.3), kind=kOutput, calls=%fused_computation.21 | convolution fusion | flops 1090781184 | bytes 20193280 | tf_op jit(solution)/shard_map/agtn,nad->agtd/dot_general | solution.py:80
  257.4 0.0 all-gather.18.cloned.1.call-update
  257.4 24.6 %all-gather.20.cloned.1.call-done = bf16[8192,256]{1,0:T(8,128)(2,1)} async-done(((bf16[1024,256]{1,0:T(8,128)(2,1)}), bf16[8192,256]{1,0:T(8,128)(2,1)}) %all-gather.20.cloned.1.call-update) | async-done | bytes 4194320 | tf_op jit(solution)/shard_map/all_gather | solution.py:97
  282.0 100.3 %all-gather.18.cloned.1.call-done = bf16[512,8192]{0,1:T(8,128)(2,1)} async-done(((bf16[512,256]{0,1:T(8,128)(2,1)}), bf16[512,8192]{0,1:T(8,128)(2,1)}) %all-gather.18.cloned.1.call-update) | async-done | bytes 8388624 | tf_op jit(solution)/shard_map/all_gather | solution.py:94
  382.4 7.7 %convolution_convert_fusion = bf16[512,256]{1,0:T(8,128)(2,1)} fusion(bf16[512,8192]{0,1:T(8,128)(2,1)} %all-gather.18.cloned.1.call-done, bf16[8192,256]{1,0:T(8,128)(2,1)} %all-gather.20.cloned.1.call-done), kind=kOutput, calls=%fused_computation.16 | convolution fusion | flops 2147614720 | bytes 12845056 | tf_op jit(solution)/shard_map/dot_general | solution.py:96
  (7 shorter events, 0.1 us)
Async XLA Ops:
  6.5 147.6 %copy-start.1 = (f32[8192]{0:T(1024)S(1)}, f32[8192]{0:T(1024)}, u32[]{:S(2)}) copy-start(f32[8192]{0:T(1024)} %param.7) | copy-start | bytes 98308
  6.5 110.6 %all-gather.8.cloned.1.call-start = ((), (), s32[]{:S(2)}) async-start(), calls=%async_computation | async-start | bytes 8650752 | tf_op jit(solution)/shard_map/all_gather | solution.py:36
  7.3 146.8 %all-gather.10.cloned.1.call-start = ((), (), s32[]{:S(2)}) async-start(), calls=%async_computation.1 | async-start | bytes 4718592 | tf_op jit(solution)/shard_map/all_gather | solution.py:55
  8.2 4.9 %collective-permute-start = (bf16[1024,2,32]{0,2,1:T(8,128)(2,1)S(1)}, bf16[1024,2,32]{0,2,1:T(8,128)(2,1)S(1)}, u32[]{:S(2)}, u32[]{:S(2)}) collective-permute-start(bf16[1024,2,32]{0,2,1:T(8,128)(2,1)S(1)} %pad_maximum_fusion.2), channel_id=1, source_target_pairs={{0,1},{1,0},{2,3},{3,2},{4,5},{5,4},{6,7},{7,6},{8,9},{9,8},{10,11... | collective-permute-start | bytes 393224 | tf_op jit(solution)/shard_map/ppermute | solution.py:10
  14.0 15.2 %collective-permute-start.1 = (bf16[1024,2,64]{0,2,1:T(8,128)(2,1)S(1)}, bf16[1024,2,64]{0,2,1:T(8,128)(2,1)S(1)}, u32[]{:S(2)}, u32[]{:S(2)}) collective-permute-start(bf16[1024,2,64]{0,2,1:T(8,128)(2,1)S(1)} %pad_maximum_fusion.1), channel_id=1, source_target_pairs={{0,2},{1,3},{2,0},{3,1},{4,6},{5,7},{6,4},{7,5},{8,10},{9,11},{10,... | collective-permute-start | bytes 786440 | tf_op jit(solution)/shard_map/ppermute | solution.py:10
  30.2 160.5 %all-gather.14.cloned.1.call-start = ((), (), s32[]{:S(2)}) async-start(), calls=%async_computation.3 | async-start | bytes 4718592 | tf_op jit(solution)/shard_map/all_gather | solution.py:50
  30.9 187.3 %all-gather.12.cloned.1.call-start = ((), (), s32[]{:S(2)}) async-start(), calls=%async_computation.2 | async-start | bytes 1179648 | tf_op jit(solution)/shard_map/all_gather | solution.py:68
  162.4 83.4 %all-gather.16.cloned.1.call-start = ((), (), s32[]{:S(2)}) async-start(), calls=%async_computation.4 | async-start | bytes 1179648 | tf_op jit(solution)/shard_map/all_gather | solution.py:69
  163.1 118.9 %all-gather.20.cloned.1.call-start = ((), (), s32[]{:S(2)}) async-start(), calls=%async_computation.6 | async-start | bytes 4718592 | tf_op jit(solution)/shard_map/all_gather | solution.py:97
  163.7 218.7 %all-gather.18.cloned.1.call-start = ((), (), s32[]{:S(2)}) async-start(), calls=%async_computation.5 | async-start | bytes 8650752 | tf_op jit(solution)/shard_map/all_gather | solution.py:94
  223.3 5.7 %copy-start = (f32[4096,512,2]{1,0,2:T(8,128)}, f32[4096,512,2]{1,0,2:T(8,128)S(1)}, u32[]{:S(2)}) copy-start(f32[4096,512,2]{1,0,2:T(8,128)S(1)} %get-tuple-element.18) | copy-start | bytes 50331652
Sparse Core Ops, SparseCore 0:
  9.8 107.2 all-gather.7
  119.0 35.0 all-gather.9
  156.0 34.6 all-gather.13
  192.3 25.8 all-gather.11
  219.9 25.7 all-gather.15
  247.5 34.5 all-gather.19
  284.6 97.6 all-gather.17
where the time goes:
time: 397 us
  waiting for transfers between devices  312 us (79%)
  matrix products  39 us (10%)
  other arithmetic  18.7 us (5%)
  between operations  13.6 us (3%)
  local copies, waits for them, and re-layouts  6.8 us (2%)
  starting transfers between devices  6.8 us (2%)
    all_gather x1, waiting for transfers between devices, per_device(): head_panel = lax.all_gather(heads, 'col', axis=1, tiled=True)  100 us
    all_gather x1, waiting for transfers between devices, per_device(): panel = lax.all_gather(hidden, 'col', axis=1, tiled=True)  86.2 us
    all_gather x1, waiting for transfers between devices, per_device(): lax.all_gather(stacked, 'row', axis=0, tiled=True)  31.8 us
    all_gather x1, waiting for transfers between devices, per_device(): lax.all_gather(wo, 'row', axis=0, tiled=True)  24.6 us
    all_gather x1, waiting for transfers between devices, per_device(): lax.all_gather(wq, 'row', axis=0, tiled=True)  23.2 us
    all_gather x1, waiting for transfers between devices, per_device(): key_piece = lax.all_gather(keys, 'row', axis=0, tiled=True)  17.7 us
    ppermute x2, waiting for transfers between devices, partner(): lax.ppermute(array, axis, [(i, i ^ 1 << distance) for i in range(lax.axis...  13.7 us
    all_gather x1, waiting for transfers between devices, per_device(): value_piece = lax.all_gather(values, 'row', axis=0, tiled=True)  12.6 us
  transfers between devices with their start and end apart: 9, of which 9 were waited for; matrix products, arithmetic and copies ran while one was open for 13% of the time, Pallas kernels for 0%

commit v1 on v0

--- a/solution.py
+++ b/solution.py
@@ -65,7 +65,9 @@
     values = pair_part[:, 1].reshape(tok_rows, kv_here, HD).astype(jnp.bfloat16)
     scale = HD ** (-0.5)
     best = jnp.full((kv_here, per_kv, tok_rows), -1e30, jnp.float32)
-    key_piece = lax.all_gather(keys, "row", axis=0, tiled=True)
+    key_piece = jnp.concatenate(
+        lax.all_to_all(jnp.stack([keys] * lax.axis_size("row")), "row", 0, 0), axis=0
+    )
     value_piece = lax.all_gather(values, "row", axis=0, tiled=True)
     count = key_piece.shape[0]
     scores = (

time: 397 us -> 381 us (0.960)
  waiting for transfers between devices: 312 us -> 291 us
  starting transfers between devices: 6.8 us -> 11 us
    all_gather x1 -> x0, waiting for transfers between devices: 17.7 us -> none  [per_device(): key_piece = lax.all_gather(keys, 'row', axis=0, tiled=True)]
    all_gather x1, waiting for transfers between devices: 12.6 us -> 2.89 us  [per_device(): value_piece = lax.all_gather(values, 'row', axis=0, tiled=True)]
    all_gather x1, waiting for transfers between devices: 23.2 us -> 29.6 us  [per_device(): lax.all_gather(wq, 'row', axis=0, tiled=True)]
    all_to_all x0 -> x1, starting transfers between devices: none -> 4.38 us  [per_device(): lax.all_to_all(jnp.stack([keys] * lax.axis_size('row')), 'row', 0, 0)]
  transfers between devices with their start and end apart: 9 -> 9, of which waited for: 9 -> 8; matrix products, arithmetic and copies ran while one was open for 13% -> 14% of each run, Pallas kernels for 0% -> 0%
where the time goes in v1:
time: 381 us; the launch traced here: 380 us
  waiting for transfers between devices  291 us (76%)
  matrix products  38.8 us (10%)
  other arithmetic  18 us (5%)
  between operations  13.6 us (4%)
  starting transfers between devices  11 us (3%)
  local copies, waits for them, and re-layouts  8.06 us (2%)
    all_gather x1, waiting for transfers between devices, per_device(): head_panel = lax.all_gather(heads, 'col', axis=1, tiled=True)  100 us
    all_gather x1, waiting for transfers between devices, per_device(): panel = lax.all_gather(hidden, 'col', axis=1, tiled=True)  86.2 us
    all_gather x1, waiting for transfers between devices, per_device(): lax.all_gather(stacked, 'row', axis=0, tiled=True)  31.8 us
    all_gather x1, waiting for transfers between devices, per_device(): lax.all_gather(wq, 'row', axis=0, tiled=True)  29.6 us
    all_gather x1, waiting for transfers between devices, per_device(): lax.all_gather(wo, 'row', axis=0, tiled=True)  24.6 us
    ppermute x2, waiting for transfers between devices, partner(): lax.ppermute(array, axis, [(i, i ^ 1 << distance) for i in range(lax.axis...  13.7 us
    dot_general x1, matrix products, per_device(): jnp.einsum('agtn,nad->agtd', probs.astype(jnp.bfloat16), value_piece, pre...  11.7 us
    dot_general x1, matrix products, per_device(): jnp.dot(columns, lax.all_gather(wo, 'row', axis=0, tiled=True), preferred...  7.66 us
  transfers between devices with their start and end apart: 9, of which 8 were waited for; matrix products, arithmetic and copies ran while one was open for 14% of the time, Pallas kernels for 0%

profile of v1, /device:TPU:1, one launch (start us, length us, event | category | flops | bytes accessed | tf_op | source)
XLA Modules:
  0.0 380.4 jit_solution(9532957552664829701)
XLA Ops:
  6.5 0.0 copy-start.1
  6.5 0.0 all-gather.7.cloned.1.call-start
  6.5 0.7 all-gather.7.cloned.1.call-update
  7.3 0.0 all-gather.9.cloned.1.call-start
  7.3 0.9 pad_maximum_fusion.2
  8.2 2.6 collective-permute-start
  10.7 2.4 collective-permute-done
  13.1 0.9 broadcast_select_fusion.3
  14.0 3.8 %collective-permute-start.1 = (bf16[1024,2,64]{0,2,1:T(8,128)(2,1)S(1)}, bf16[1024,2,64]{0,2,1:T(8,128)(2,1)S(1)}, u32[]{:S(2)}, u32[]{:S(2)}) collective-permute-start(bf16[1024,2,64]{0,2,1:T(8,128)(2,1)S(1)} %pad_maximum_fusion.1), channel_id=1, source_target_pairs={{0,2},{1,3},{2,0},{3,1},{4,6},{5,7},{6,4},{7,5},{8,10},{9,11},{10,... | collective-permute-start | bytes 786440 | tf_op jit(solution)/shard_map/ppermute | solution.py:10
  17.9 11.3 %collective-permute-done.1 = bf16[1024,2,64]{0,2,1:T(8,128)(2,1)S(1)} collective-permute-done((bf16[1024,2,64]{0,2,1:T(8,128)(2,1)S(1)}, bf16[1024,2,64]{0,2,1:T(8,128)(2,1)S(1)}, u32[]{:S(2)}, u32[]{:S(2)}) %collective-permute-start.1) | collective-permute-done | bytes 262176 | tf_op jit(solution)/shard_map/ppermute | solution.py:10
  29.2 0.1 broadcast_select_fusion.1
  29.3 0.8 pad_maximum_fusion
  30.2 0.0 all-gather.9.cloned.1.call-update
  30.2 0.0 all-gather.11.cloned.1.call-start
  30.2 0.7 all-gather.11.cloned.1.call-update
  30.9 0.0 all-gather.13.cloned.1.call-start
  31.0 86.2 %all-gather.7.cloned.1.call-done = bf16[512,8192]{1,0:T(8,128)(2,1)} async-done(((bf16[512,256]{1,0:T(8,128)(2,1)}), bf16[512,8192]{1,0:T(8,128)(2,1)}) %all-gather.7.cloned.1.call-update) | async-done | bytes 8388624 | tf_op jit(solution)/shard_map/all_gather | solution.py:36
  117.1 5.1 %fusion = f32[512]{0:T(512)S(1)} fusion(bf16[512,8192]{1,0:T(8,128)(2,1)} %all-gather.7.cloned.1.call-done), kind=kLoop, calls=%fused_computation.2 | loop fusion | flops 12582400 | bytes 8390656 | tf_op jit(solution)/shard_map/reduce_sum | solution.py:38
  122.3 31.8 %all-gather.9.cloned.1.call-done = bf16[8192,2,128]{0,2,1:T(8,128)(2,1)} async-done(((bf16[1024,2,128]{0,2,1:T(8,128)(2,1)}), bf16[8192,2,128]{0,2,1:T(8,128)(2,1)}) %all-gather.9.cloned.1.call-update) | async-done | bytes 4194320 | tf_op jit(solution)/shard_map/all_gather | solution.py:55
  154.1 0.0 copy-done.1
  154.1 7.0 %fusion.12 = f32[512,256]{0,1:S(1)} fusion(bf16[8192,256]{0,1:T(8,128)(2,1)} %bitcast.62, bf16[512,8192]{1,0:T(8,128)(2,1)} %all-gather.7.cloned.1.call-done, f32[8192]{0:T(1024)S(1)} %copy-done.1, f32[512]{0:T(512)S(1)} %add_rsqrt_fusion), kind=kOutput, calls=%fused_computation.15 | convolution fusion | flops 2164260864 | bytes 13142016
  161.1 0.7 slice.42
  161.8 0.0 all-gather.13.cloned.1.call-update
  161.8 0.0 all-gather.17.cloned.1.call-start
  161.9 0.5 all-gather.17.cloned.1.call-update
  162.5 1.8 multiply_cosine_fusion
  164.3 1.7 iota_compare_fusion
  166.0 0.6 fusion.38
  166.6 0.1 copy.11
  166.7 1.1 stack.11
  167.8 4.4 %all-to-all-start = ((bf16[8,512,1,128]{3,1,2,0:T(8,128)(2,1)}), bf16[8,512,1,128]{3,1,2,0:T(8,128)(2,1)}, u32[]{:S(2)}, u32[]{:S(2)}) async-start(bf16[8,512,1,128]{3,1,2,0:T(8,128)(2,1)} %stack.11), calls=%async_computation | async-start | bytes 2097152 | tf_op jit(solution)/shard_map/all_to_all | solution.py:69
  172.2 0.1 all-gather.15.cloned.1.call-start
  172.3 29.6 %all-gather.11.cloned.1.call-done = bf16[8192,256]{1,0:T(8,128)(2,1)} async-done(((bf16[1024,256]{1,0:T(8,128)(2,1)}), bf16[8192,256]{1,0:T(8,128)(2,1)}) %all-gather.11.cloned.1.call-update) | async-done | bytes 4194320 | tf_op jit(solution)/shard_map/all_gather | solution.py:50
  201.9 7.6 %fusion.10 = f32[512,256]{0,1:T(8,128)S(1)} fusion(bf16[8192,256]{1,0:T(8,128)(2,1)} %all-gather.11.cloned.1.call-done, bf16[512,8192]{1,0:T(8,128)(2,1)} %all-gather.7.cloned.1.call-done, f32[8192]{0:T(1024)S(1)} %copy-done.1, f32[512]{0:T(512)S(1)} %add_rsqrt_fusion), kind=kOutput, calls=%fused_computation.14 | convolution fusion | flops 2164260864 | bytes 13142016 | tf_op jit(solution)/shard_map/dot_general | solution.py:49
  209.5 0.2 copy.16
  209.7 0.2 copy.17
  209.9 1.9 subtract_convert_fusion
  211.8 0.0 all-to-all-done
  211.8 4.9 %fusion.5 = (f32[2,512]{1,0:T(2,128)S(1)}, f32[4096,512,2]{1,0,2:T(8,128)S(1)}) fusion(pred[512,4096]{0,1:T(8,128)(4,1)S(1)} %iota_compare_fusion, bf16[4096,128,1]{1,0,2:T(8,128)(2,1)} %bitcast.7, bf16[512,2,64]{2,0,1:T(8,128)(2,1)} %get-tuple-element.6, bf16[512,2,64]{2,0,1:T(8,128)(2,1)S(1)} %get-tuple-element.5), kind=kOutput, calls=%fused_computation.9 | convolution fusion | flops 1086848000 | bytes 20189184 | tf_op jit(solution)/shard_map/tagd,nad->agtn/dot_general | solution.py:74
  216.7 0.0 copy-start
  216.7 5.7 %copy-done = f32[4096,512,2]{1,0,2:T(8,128)} copy-done((f32[4096,512,2]{1,0,2:T(8,128)}, f32[4096,512,2]{1,0,2:T(8,128)S(1)}, u32[]{:S(2)}) %copy-start) | copy-done | bytes 16777240
  222.4 4.2 %fusion.3 = f32[2,512]{1,0:T(2,128)S(1)} fusion(f32[4096,512,2]{1,0,2:T(8,128)S(1)} %get-tuple-element.18, f32[2,512]{1,0:T(2,128)S(1)} %broadcast_maximum_fusion, pred[512,4096]{0,1:T(8,128)(4,1)S(1)} %iota_compare_fusion), kind=kLoop, calls=%fused_computation.7 | loop fusion | flops 16776192 | bytes 18882560 | tf_op jit(solution)/shard_map/reduce_sum | solution.py:81
  226.6 2.9 all-gather.13.cloned.1.call-done
  229.5 11.7 %fusion.20 = bf16[2,512,128]{1,2,0:T(8,128)(2,1)} fusion(f32[4096,512,2]{1,0,2:T(8,128)} %copy-done, f32[2,512]{1,0:T(2,128)S(1)} %broadcast_maximum_fusion, pred[512,4096]{0,1:T(8,128)(4,1)S(1)} %iota_compare_fusion, bf16[4096,1,128]{0,2,1:T(8,128)(2,1)} %all-gather.13.cloned.1.call-done, f32[2,512]{1,0:T(2,128)S(1)} %fusion.3), kind=kOutput, calls=%fused_computation.19 | convolution fusion | flops 1090781184 | bytes 20193280 | tf_op jit(solution)/shard_map/agtn,nad->agtd/dot_general | solution.py:82
  241.1 0.0 all-gather.15.cloned.1.call-update
  241.2 24.6 %all-gather.17.cloned.1.call-done = bf16[8192,256]{1,0:T(8,128)(2,1)} async-done(((bf16[1024,256]{1,0:T(8,128)(2,1)}), bf16[8192,256]{1,0:T(8,128)(2,1)}) %all-gather.17.cloned.1.call-update) | async-done | bytes 4194320 | tf_op jit(solution)/shard_map/all_gather | solution.py:99
  265.8 100.2 %all-gather.15.cloned.1.call-done = bf16[512,8192]{0,1:T(8,128)(2,1)} async-done(((bf16[512,256]{0,1:T(8,128)(2,1)}), bf16[512,8192]{0,1:T(8,128)(2,1)}) %all-gather.15.cloned.1.call-update) | async-done | bytes 8388624 | tf_op jit(solution)/shard_map/all_gather | solution.py:96
  365.9 7.7 %convolution_convert_fusion = bf16[512,256]{1,0:T(8,128)(2,1)} fusion(bf16[512,8192]{0,1:T(8,128)(2,1)} %all-gather.15.cloned.1.call-done, bf16[8192,256]{1,0:T(8,128)(2,1)} %all-gather.17.cloned.1.call-done), kind=kOutput, calls=%fused_computation.16 | convolution fusion | flops 2147614720 | bytes 12845056 | tf_op jit(solution)/shard_map/dot_general | solution.py:98
  (8 shorter events, 0.1 us)
Async XLA Ops:
  6.5 147.6 %copy-start.1 = (f32[8192]{0:T(1024)S(1)}, f32[8192]{0:T(1024)}, u32[]{:S(2)}) copy-start(f32[8192]{0:T(1024)} %param.7) | copy-start | bytes 98308
  6.5 110.6 %all-gather.7.cloned.1.call-start = ((), (), s32[]{:S(2)}) async-start(), calls=%async_computation.1 | async-start | bytes 8650752 | tf_op jit(solution)/shard_map/all_gather | solution.py:36
  7.3 146.8 %all-gather.9.cloned.1.call-start = ((), (), s32[]{:S(2)}) async-start(), calls=%async_computation.2 | async-start | bytes 4718592 | tf_op jit(solution)/shard_map/all_gather | solution.py:55
  8.2 4.9 %collective-permute-start = (bf16[1024,2,32]{0,2,1:T(8,128)(2,1)S(1)}, bf16[1024,2,32]{0,2,1:T(8,128)(2,1)S(1)}, u32[]{:S(2)}, u32[]{:S(2)}) collective-permute-start(bf16[1024,2,32]{0,2,1:T(8,128)(2,1)S(1)} %pad_maximum_fusion.2), channel_id=1, source_target_pairs={{0,1},{1,0},{2,3},{3,2},{4,5},{5,4},{6,7},{7,6},{8,9},{9,8},{10,11... | collective-permute-start | bytes 393224 | tf_op jit(solution)/shard_map/ppermute | solution.py:10
  14.0 15.2 %collective-permute-start.1 = (bf16[1024,2,64]{0,2,1:T(8,128)(2,1)S(1)}, bf16[1024,2,64]{0,2,1:T(8,128)(2,1)S(1)}, u32[]{:S(2)}, u32[]{:S(2)}) collective-permute-start(bf16[1024,2,64]{0,2,1:T(8,128)(2,1)S(1)} %pad_maximum_fusion.1), channel_id=1, source_target_pairs={{0,2},{1,3},{2,0},{3,1},{4,6},{5,7},{6,4},{7,5},{8,10},{9,11},{10,... | collective-permute-start | bytes 786440 | tf_op jit(solution)/shard_map/ppermute | solution.py:10
  30.2 171.7 %all-gather.11.cloned.1.call-start = ((), (), s32[]{:S(2)}) async-start(), calls=%async_computation.3 | async-start | bytes 4718592 | tf_op jit(solution)/shard_map/all_gather | solution.py:50
  30.9 198.6 %all-gather.13.cloned.1.call-start = ((), (), s32[]{:S(2)}) async-start(), calls=%async_computation.4 | async-start | bytes 1179648 | tf_op jit(solution)/shard_map/all_gather | solution.py:71
  161.8 103.9 %all-gather.17.cloned.1.call-start = ((), (), s32[]{:S(2)}) async-start(), calls=%async_computation.6 | async-start | bytes 4718592 | tf_op jit(solution)/shard_map/all_gather | solution.py:99
  167.8 44.0 %all-to-all-start = ((bf16[8,512,1,128]{3,1,2,0:T(8,128)(2,1)}), bf16[8,512,1,128]{3,1,2,0:T(8,128)(2,1)}, u32[]{:S(2)}, u32[]{:S(2)}) async-start(bf16[8,512,1,128]{3,1,2,0:T(8,128)(2,1)} %stack.11), calls=%async_computation | async-start | bytes 2097152 | tf_op jit(solution)/shard_map/all_to_all | solution.py:69
  172.2 193.7 %all-gather.15.cloned.1.call-start = ((), (), s32[]{:S(2)}) async-start(), calls=%async_computation.5 | async-start | bytes 8650752 | tf_op jit(solution)/shard_map/all_gather | solution.py:96
  216.7 5.7 %copy-start = (f32[4096,512,2]{1,0,2:T(8,128)}, f32[4096,512,2]{1,0,2:T(8,128)S(1)}, u32[]{:S(2)}) copy-start(f32[4096,512,2]{1,0,2:T(8,128)S(1)} %get-tuple-element.18) | copy-start | bytes 50331652
Sparse Core Ops, SparseCore 0:
  9.8 107.2 all-gather.6
  119.0 35.0 all-gather.8
  156.0 45.8 all-gather.10
  203.6 25.8 all-gather.12
  231.2 34.5 all-gather.16
  268.2 97.6 all-gather.14
